TPU v7x, 32 devices: a whole 2x2x4 slice. The times are simulated.
32 devices in a mesh: people: 8 (over z, x), var: 4 (over y, core).
Axes of the slice: x: 2, y: 2, z: 4, core: 2. Of those that a mesh axis runs over, the one named last changes fastest.
Arguments:
- genotypes: bfloat16 [4096, 2048], P('people', 'var'), may hold values from -6 to 6
- kin_diag: bfloat16 [16, 256, 256], P('people'), may hold values from -0.375 to 0.375
- kin_blocks: bfloat16 [256, 256, 256], P('people'), may hold values from -0.375 to 0.375
- kin_pairs: int32 [256, 2], replicated, may hold values from 0 to 15, as said below
- pair_count: int32 [8], replicated, may hold values from 24 to 32, as said below
- gene_counts: int32 [64], replicated, may hold values from 1 to 1024, 2048 in all
Outputs:
- gene_variance: float32 [2048, 2048], P(('var', 'people'))
Inputs may be any that keep to these rules, and one draw needn't show every extreme that they name: `kin_pairs`: slots 32 d to 32 d + 31 belong to index d of people: their row block is one of d's blocks d * 2 to d * 2 + 1, their column block is held by another index of people, and among d's live slots at most 5 slots name column blocks held by any one index; some index of people reaches 5 with one index. `pair_count`: some index of people has all 32 slots live.
All inputs are finite; a program needn't handle non-finite values.
Results may differ from a plain program's by a relative error of at most 0.0029.
Values may be sent and summed in bfloat16 or wider, within the bound.
A program may use at most 128 MiB of HBM per device.

v0:
```python
import math

import jax
import jax.numpy as jnp
from jax import lax
from jax.sharding import PartitionSpec as P

BLOCK = 256


def gene_index(positions, gene_counts):
    gene_ends = jnp.cumsum(gene_counts)
    return jnp.sum((positions[:, None] >= gene_ends[None, :]).astype(jnp.int32), axis=1)


def body(genotypes, kin_diag, kin_blocks, kin_pairs, pair_count, gene_counts):
    row_count, col_count = genotypes.shape
    people = lax.axis_size("people")
    my_index = lax.axis_index("people")
    block_count = row_count // BLOCK
    pair_slots = kin_blocks.shape[0]
    geno_blocks = genotypes.reshape(block_count, BLOCK, col_count)
    kin_times = jnp.einsum(
        "bij,bjv->biv", kin_diag, geno_blocks, preferred_element_type=jnp.float32
    )
    pair_table = kin_pairs.reshape(people, pair_slots, 2)
    row_all = pair_table[:, :, 0]
    col_all = pair_table[:, :, 1]
    slot_ids = jnp.arange(pair_slots, dtype=jnp.int32)
    live_all = slot_ids[None, :] < pair_count[:, None]
    my_rows = lax.dynamic_index_in_dim(row_all, my_index, 0, keepdims=False)
    my_cols = lax.dynamic_index_in_dim(col_all, my_index, 0, keepdims=False)
    my_live = lax.dynamic_index_in_dim(live_all, my_index, 0, keepdims=False)
    wanted = my_cols[:, None] * BLOCK + jnp.arange(BLOCK, dtype=jnp.int32)[None, :]
    empty_rows = jnp.zeros((pair_slots, BLOCK, col_count), jnp.bfloat16)
    shard_rows = lax.all_gather(genotypes, "people", axis=0, tiled=True)
    row_span = shard_rows.shape[0]
    inside = (wanted >= 0) & (wanted < row_span)
    picked = jnp.take(shard_rows, jnp.clip(wanted, 0, row_span - 1).reshape(-1), axis=0)
    picked = picked.reshape(pair_slots, BLOCK, col_count)
    fetched = jnp.where(inside[:, :, None], picked, empty_rows)
    pair_terms = jnp.einsum("jab,jbv->jav", kin_blocks, fetched, preferred_element_type=jnp.float32)
    home_block = my_rows % block_count
    placing = (home_block[:, None] == jnp.arange(block_count, dtype=jnp.int32)[None, :]).astype(
        jnp.float32
    )
    placing = placing * my_live.astype(jnp.float32)[:, None]
    kin_times = kin_times + jnp.einsum(
        "jr,jav->rav", placing, pair_terms, precision=lax.Precision.HIGHEST
    )
    kin_rounded = kin_times.reshape(row_count, col_count).astype(jnp.bfloat16)
    stacked = jnp.stack([genotypes, kin_rounded])
    shard_cols = lax.all_gather(stacked, "var", axis=2, tiled=True)
    own_geno = jnp.einsum("pv,pw->vw", genotypes, shard_cols[1], preferred_element_type=jnp.float32)
    own_kin = jnp.einsum(
        "pv,pw->vw", kin_rounded, shard_cols[0], preferred_element_type=jnp.float32
    )
    partial_value = (own_geno + own_kin) * 0.5
    variant_total = col_count * lax.axis_size("var")
    persons = row_count * people
    scaling = 1.0 / math.sqrt(persons)
    my_vars = lax.axis_index("var") * col_count + jnp.arange(col_count, dtype=jnp.int32)
    row_genes = gene_index(my_vars, gene_counts)
    col_genes = gene_index(jnp.arange(variant_total, dtype=jnp.int32), gene_counts)
    same_gene = row_genes[:, None] == col_genes[None, :]
    partial_value = jnp.where(same_gene, partial_value * scaling, jnp.float32(0.0))
    result = lax.psum_scatter(partial_value, "people", scatter_dimension=0, tiled=True)
    return result


def solution(mesh):
    placed = (P("people", "var"), P("people", None, None), P("people", None, None), P(), P(), P())
    return jax.shard_map(
        body, mesh=mesh, in_specs=placed, out_specs=P(("var", "people"), None), check_vma=False
    )
```

profile of v0, /device:TPU:26, one launch (start us, length us, event | category | flops | bytes accessed | tf_op | source)
XLA Modules:
  0.0 316.0 jit_solution(12974185727075465695)
XLA Ops:
  6.5 0.0 copy-start
  6.5 0.0 all-gather.3.cloned.1.call-start
  6.5 0.7 all-gather.3.cloned.1.call-update
  7.3 0.0 all-gather.5.cloned.1.call-start
  7.3 0.8 reshape.168
  8.1 0.1 fusion.13
  8.2 0.7 iota_compare_fusion.1
  9.0 0.1 fusion.17
  9.1 72.1 %all-gather.3.cloned.1.call-done = bf16[4096,512]{1,0:T(8,128)(2,1)} async-done(((bf16[512,512]{1,0:T(8,128)(2,1)}), bf16[4096,512]{1,0:T(8,128)(2,1)}) %all-gather.3.cloned.1.call-update) | async-done | bytes 4194320 | tf_op jit(solution)/shard_map/all_gather | solution.py:36
  81.2 36.7 %gather_fusion = bf16[8192,512]{1,0:T(8,128)(2,1)} fusion(bf16[4096,512]{1,0:T(8,128)(2,1)} %all-gather.3.cloned.1.call-done, s32[8192]{0:T(1024)S(1)} %broadcast_clamp_fusion), kind=kCustom, calls=%fused_computation | custom fusion | bytes 16809984 | tf_op jit(solution)/shard_map/jit(_take)/gather | solution.py:39
  117.9 11.9 %copy.30 = bf16[32,256,512]{1,2,0:T(8,128)(2,1)} copy(bf16[32,256,512]{2,1,0:T(8,128)(2,1)} %bitcast.58) | data formatting | bytes 16777216 | tf_op jit(solution)/shard_map/jit(_take)/gather | solution.py:39
  129.9 12.7 %convolution_bitcast_fusion = f32[32,256,512]{1,2,0:T(8,128)} fusion(bf16[32,256,256]{2,1,0:T(8,128)(2,1)} %param.8, bf16[32,256,512]{1,2,0:T(8,128)(2,1)} %copy.30, pred[32,256]{1,0:T(8,128)(4,1)S(1)} %get-tuple-element.8, pred[32,256]{1,0:T(8,128)(4,1)S(1)} %get-tuple-element.7), kind=kOutput, calls=%fused_computation.1 | convolution fusion | flops 2155872256 | bytes 29376512 | tf_op jit(solution)/shard_map/jab,jbv->jav/dot_general | solution.py:42
  142.5 20.3 %copy.31 = f32[32,256,512]{2,0,1:T(8,128)} copy(f32[32,256,512]{1,2,0:T(8,128)} %convolution_bitcast_fusion) | data formatting | bytes 33554432 | tf_op jit(solution)/shard_map/jab,jbv->jav/dot_general | solution.py:42
  162.8 11.0 %fusion.19 = f32[2,256,512]{2,0,1:T(2,128)S(1)} fusion(f32[32,256,512]{2,0,1:T(8,128)} %copy.31, f32[32]{0:T(128)S(1)} %fusion.26, s32[32]{0:T(128)S(1)} %and_select_fusion), kind=kOutput, calls=%fused_computation.40 | convolution fusion | flops 100663424 | bytes 17826048 | tf_op jit(solution)/shard_map/jr,jav->rav/dot_general | solution.py:48
  173.8 0.0 copy-start.3
  173.8 0.0 copy-done
  173.8 0.0 copy-done.1
  173.8 0.3 fusion.9
  174.2 1.1 pad_maximum_fusion
  175.2 0.0 all-gather.5.cloned.1.call-update
  175.2 0.0 reduce-scatter.4.cloned.1.call-start
  175.3 0.1 copy.27
  175.4 0.1 reduce-window.8
  175.5 0.1 reduce
  175.6 0.1 convert_reduce_fusion.1
  175.7 0.1 convert_reduce_fusion
  175.9 34.9 %all-gather.5.cloned.1.call-done = bf16[2,512,2048]{2,1,0:T(8,128)(2,1)} async-done(((bf16[2,512,512]{2,1,0:T(8,128)(2,1)}), bf16[2,512,2048]{2,1,0:T(8,128)(2,1)}) %all-gather.5.cloned.1.call-update) | async-done | bytes 4194320 | tf_op jit(solution)/shard_map/all_gather | solution.py:53
  210.8 3.0 fusion.8
  213.9 2.9 fusion.5
  216.7 5.5 %copy.36 = f32[512,2048]{1,0:T(8,128)} copy(f32[512,2048]{0,1:T(8,128)} %fusion.5) | data formatting | bytes 8388608
  222.2 0.0 reduce-scatter.4.cloned.1.call-update
  222.2 87.3 %reduce-scatter.4.cloned.1.call-done = f32[64,2048]{1,0:T(8,128)} async-done(((f32[512,2048]{1,0:T(8,128)}), f32[64,2048]{1,0:T(8,128)}) %reduce-scatter.4.cloned.1.call-update) | async-done | bytes 524304 | tf_op jit(solution)/shard_map/reduce_scatter | solution.py:67
  (12 shorter events, 0.1 us)
Async XLA Ops:
  6.5 167.3 %copy-start = (bf16[2,256,256]{2,1,0:T(8,128)(2,1)S(1)}, bf16[2,256,256]{2,1,0:T(8,128)(2,1)}, u32[]{:S(2)}) copy-start(bf16[2,256,256]{2,1,0:T(8,128)(2,1)} %param.7) | copy-start | bytes 786436
  6.5 74.7 %all-gather.3.cloned.1.call-start = ((), (), s32[]{:S(2)}) async-start(), calls=%async_computation.1 | async-start | bytes 4718592 | tf_op jit(solution)/shard_map/all_gather | solution.py:36
  7.3 203.6 %all-gather.5.cloned.1.call-start = ((), (), s32[]{:S(2)}) async-start(), calls=%async_computation.2 | async-start | bytes 5242880 | tf_op jit(solution)/shard_map/all_gather | solution.py:53
  162.8 11.0 %copy-start.1 = (bf16[512,512]{1,0:T(8,128)(2,1)S(1)}, bf16[512,512]{1,0:T(8,128)(2,1)}, u32[]{:S(2)}) copy-start(bf16[512,512]{1,0:T(8,128)(2,1)} %param.6) | copy-start | bytes 1572868
  173.8 1.5 copy-start.3
  175.2 134.3 %reduce-scatter.4.cloned.1.call-start = ((), (), s32[]{:S(2)}) async-start(), calls=%async_computation.3 | async-start | bytes 4718592 | tf_op jit(solution)/shard_map/reduce_scatter | solution.py:67
  210.8 3.0 copy-start.2
Sparse Core Ops, SparseCore 0:
  9.5 71.6 all-gather.2
  175.4 35.3 all-gather.4
  222.3 87.1 reduce-scatter.3
where the time goes:
time: 320 us; the launch traced here: 316 us
  waiting for transfers between devices  195 us (61%)
  local copies, waits for them, and re-layouts  75.3 us (24%)
  matrix products  29.9 us (9%)
  between operations  13.2 us (4%)
    reduce_scatter x1, waiting for transfers between devices, body(): lax.psum_scatter(partial_value, 'people', scatter_dimension=0, tiled=True)  87.3 us
    all_gather x1, waiting for transfers between devices, body(): shard_rows = lax.all_gather(genotypes, 'people', axis=0, tiled=True)  72.1 us
    gather x2, local copies, waits for them, and re-layouts, body(): jnp.take(shard_rows, jnp.clip(wanted, 0, row_span - 1).reshape(-1), axis=0)  48.6 us
    all_gather x1, waiting for transfers between devices, body(): shard_cols = lax.all_gather(stacked, 'var', axis=2, tiled=True)  34.9 us
    dot_general x1, local copies, waits for them, and re-layouts, body(): jnp.einsum('jab,jbv->jav', kin_blocks, fetched, preferred_element_type=jn...  20.3 us
    dot_general x1, matrix products, body(): jnp.einsum('jab,jbv->jav', kin_blocks, fetched, preferred_element_type=jn...  12.7 us
    dot_general x1, matrix products, body(): jnp.einsum('jr,jav->rav', placing, pair_terms, precision=lax.Precision.HI...  11 us
  transfers between devices with their start and end apart: 3, of which 3 were waited for; matrix products, arithmetic and copies ran while one was open for 1% of the time, Pallas kernels for 0%

commit v1 on v0

v1 whole, which is shorter than its diff:
```python
import functools
import math

import jax
import jax.numpy as jnp
from jax import lax
from jax.experimental import pallas as pl
from jax.experimental.pallas import tpu as pltpu
from jax.sharding import PartitionSpec as P

BLOCK = 256
SUB = 2
CORES = 2
MESH = pl.DeviceIdType.MESH


def ring_place(index, nz, nx):
    z, x = index // nx, index % nx
    back = nz - 1 - z
    along = jnp.where(back % 2 == 0, x - 1, nx - 1 - x)
    return jnp.where(x == 0, z, nz + back * (nx - 1) + along)


def ring_index(place, nz, nx):
    rest = jnp.where(place < nz, 0, place - nz)
    back, along = rest // (nx - 1), rest % (nx - 1)
    x = jnp.where(back % 2 == 0, 1 + along, nx - 1 - along)
    return jnp.where(place < nz, place * nx, (nz - 1 - back) * nx + x)


def kernel(people, var, g_ref, kd_hbm, kb_hbm, pairs_hbm, cnt_ref, gc_ref, out_ref,
           gall, gvar, krv, kd, kb, acc, g_t, kr_t, pbuf, rbuf, rid, cid, pairs_s,
           ring_send, ring_recv, var_send, var_recv, sum_send, sum_recv, load_sem):
    rows, cols = g_ref.shape
    nx = math.isqrt(people // 2)
    nz = people // nx
    ny = var // CORES
    slots = kb.shape[0]
    me, q = lax.axis_index("people"), lax.axis_index("var")
    y, core = q // CORES, q % CORES
    other = y * CORES + (CORES - 1 - core)

    loads = [
        pltpu.make_async_copy(pairs_hbm.at[pl.ds(me * slots, slots)], pairs_s, load_sem.at[0]),
        pltpu.make_async_copy(kd_hbm, kd, load_sem.at[1]),
        pltpu.make_async_copy(kb_hbm, kb, load_sem.at[2]),
    ]
    for load in loads:
        load.start()

    barrier = pltpu.get_barrier_semaphore()
    for step in range(1, people):
        pl.semaphore_signal(barrier, inc=1, device_id=(lax.rem(me + step, people), q), device_id_type=MESH)
    for step in range(1, var):
        pl.semaphore_signal(barrier, inc=1, device_id=(me, lax.rem(q + step, var)), device_id_type=MESH)
    pl.semaphore_wait(barrier, people + var - 2)

    place = ring_place(me, nz, nx)
    right = ring_index(lax.rem(place + 1, people), nz, nx)
    left = ring_index(lax.rem(place + people - 1, people), nz, nx)
    part = BLOCK // SUB

    def ring_copy(step, way, sub):
        shift = people - step if way == 0 else step
        source = ring_index(lax.rem(place + shift, people), nz, nx)
        view = gall.at[2 * source + way, pl.ds(sub * part, part)]
        return pltpu.make_async_remote_copy(
            src_ref=view, dst_ref=view,
            send_sem=ring_send.at[step, way, sub], recv_sem=ring_recv.at[step, way, sub],
            device_id=(right if way == 0 else left, q), device_id_type=MESH)

    def var_copy(buf, use, slot, target, sem):
        return pltpu.make_async_remote_copy(
            src_ref=buf.at[slot], dst_ref=buf.at[slot],
            send_sem=var_send.at[use, sem], recv_sem=var_recv.at[use, sem],
            device_id=(me, target), device_id_type=MESH)

    def var_first(buf, use):
        for dy in range(1, ny):
            var_copy(buf, use, q, lax.rem(y + dy, ny) * CORES + core, dy - 1).start()
        var_copy(buf, use, q, other, ny - 1).start()

    def var_forward(buf, use):
        for dy in range(1, ny):
            slot = lax.rem(y + ny - dy, ny) * CORES + core
            var_copy(buf, use, slot, other, dy - 1).wait_recv()
            var_copy(buf, use, slot, other, ny - 1 + dy).start()

    def var_finish(buf, use):
        for sem in range(ny - 1, 2 * ny - 1):
            var_copy(buf, use, q, other, sem).wait_recv()
        for sem in range(2 * ny - 1):
            var_copy(buf, use, q, other, sem).wait_send()

    for half in range(rows // BLOCK):
        gall[2 * me + half] = g_ref[pl.ds(half * BLOCK, BLOCK), :]
    gvar[q] = g_ref[...]
    for sub in range(SUB):
        for way in range(2):
            ring_copy(0, way, sub).start()
    var_first(gvar, 0)

    g_t[...] = g_ref[...].T
    rid[...] = jnp.zeros_like(rid)
    cid[...] = jnp.zeros_like(cid)

    def gene_step(gene, end):
        end = end + gc_ref[gene]
        row_ids = q * cols + lax.broadcasted_iota(jnp.int32, rid.shape, 0)
        col_ids = lax.broadcasted_iota(jnp.int32, cid.shape, 1)
        rid[...] += (row_ids >= end).astype(jnp.int32)
        cid[...] += (col_ids >= end).astype(jnp.int32)
        return end

    lax.fori_loop(0, gc_ref.shape[0], gene_step, jnp.int32(0))

    def ring_step(step, carry):
        for sub in range(SUB):
            for way in range(2):
                ring_copy(step - 1, way, sub).wait_recv()
                ring_copy(step, way, sub).start()
        return carry

    lax.fori_loop(1, people - 1, ring_step, 0)
    var_forward(gvar, 0)
    for load in loads:
        load.wait()
    for half in range(rows // BLOCK):
        acc[half] = jnp.dot(kd[half], g_ref[pl.ds(half * BLOCK, BLOCK), :], preferred_element_type=jnp.float32)
    for sub in range(SUB):
        for way in range(2):
            ring_copy(people - 2, way, sub).wait_recv()

    def pair_step(slot, carry):
        row = pairs_s[slot, 0] - me * 2
        col = pairs_s[slot, 1]
        live = slot < cnt_ref[me]
        term = jnp.dot(kb[slot], gall[col], preferred_element_type=jnp.float32)
        for half in range(2):
            weight = jnp.where(live & (row == half), 1.0, 0.0).astype(jnp.float32)
            acc[half] += term * weight
        return carry

    lax.fori_loop(0, slots, pair_step, 0)
    for half in range(2):
        krv[q, pl.ds(half * BLOCK, BLOCK), :] = acc[half].astype(jnp.bfloat16)
    var_first(krv, 1)
    kr_t[...] = krv[q].T

    def ring_drain(step, carry):
        for sub in range(SUB):
            for way in range(2):
                ring_copy(step, way, sub).wait_send()
        return carry

    lax.fori_loop(0, people - 1, ring_drain, 0)
    var_finish(gvar, 0)
    var_forward(krv, 1)
    var_finish(krv, 1)

    width = pbuf.shape[2]
    chunk = rows // people
    tile = BLOCK
    per_tile = tile // chunk

    def sum_copy(target):
        return pltpu.make_async_remote_copy(
            src_ref=pbuf.at[target], dst_ref=rbuf.at[me],
            send_sem=sum_send.at[target], recv_sem=sum_recv.at[me],
            device_id=(target, q), device_id_type=MESH)

    for t in range(cols // tile):
        span = pl.ds(t * tile, tile)
        row_gene = rid[span, 0:1]
        for j in range(var // 2):
            total = jnp.zeros((tile, cols), jnp.float32)
            for k in (j, j + var // 2):
                value = jnp.dot(g_t[span, :], krv[k], preferred_element_type=jnp.float32)
                value += jnp.dot(kr_t[span, :], gvar[k], preferred_element_type=jnp.float32)
                same = row_gene == cid[0:1, k * cols:(k + 1) * cols]
                total = jnp.where(same, value, total)
            pbuf[t * per_tile:(t + 1) * per_tile, :, j * cols:(j + 1) * cols] = (
                total.astype(jnp.bfloat16).reshape(per_tile, chunk, cols))
        for k in range(per_tile):
            target = t * per_tile + k

            @pl.when(target != me)
            def _():
                sum_copy(target).start()

    own = rid[pl.ds(me * chunk, chunk), 0:1]
    final = pbuf[me].astype(jnp.float32)
    for step in range(1, people):
        source = lax.rem(me + step, people)
        pltpu.make_async_remote_copy(
            src_ref=pbuf.at[source], dst_ref=rbuf.at[source],
            send_sem=sum_send.at[source], recv_sem=sum_recv.at[source],
            device_id=(source, q), device_id_type=MESH).wait_recv()
        final += rbuf[source].astype(jnp.float32)
    final = final * (0.5 / math.sqrt(rows * people))
    for k in range(2):
        same = own == cid[0:1, k * width:(k + 1) * width]
        out_ref[:, k * width:(k + 1) * width] = jnp.where(same, final, 0.0)
    for step in range(1, people):
        sum_copy(lax.rem(me + step, people)).wait_send()


def body(people, var, genotypes, kin_diag, kin_blocks, kin_pairs, pair_count, gene_counts):
    rows, cols = genotypes.shape
    slots = kin_blocks.shape[0]
    total = cols * var
    chunk = rows // people
    ny = var // CORES
    bf16, f32 = jnp.bfloat16, jnp.float32
    anywhere = pl.BlockSpec(memory_space=pl.ANY)
    vmem = pl.BlockSpec(memory_space=pltpu.VMEM)
    smem = pl.BlockSpec(memory_space=pltpu.SMEM)
    dma = pltpu.SemaphoreType.DMA
    return pl.pallas_call(
        functools.partial(kernel, people, var),
        out_shape=jax.ShapeDtypeStruct((chunk, total), f32),
        in_specs=[vmem, anywhere, anywhere, anywhere, smem, smem],
        out_specs=vmem,
        scratch_shapes=[
            pltpu.VMEM((2 * people, BLOCK, cols), bf16),
            pltpu.VMEM((var, rows, cols), bf16),
            pltpu.VMEM((var, rows, cols), bf16),
            pltpu.VMEM(kin_diag.shape, bf16),
            pltpu.VMEM(kin_blocks.shape, bf16),
            pltpu.VMEM((2, BLOCK, cols), f32),
            pltpu.VMEM((cols, rows), bf16),
            pltpu.VMEM((cols, rows), bf16),
            pltpu.VMEM((people, chunk, total // 2), bf16),
            pltpu.VMEM((people, chunk, total // 2), bf16),
            pltpu.VMEM((cols, 128), jnp.int32),
            pltpu.VMEM((8, total), jnp.int32),
            pltpu.SMEM((slots, 2), jnp.int32),
            dma((people - 1, 2, SUB)),
            dma((people - 1, 2, SUB)),
            dma((2, 2 * ny - 1)),
            dma((2, 2 * ny - 1)),
            dma((people,)),
            dma((people,)),
            dma((3,)),
        ],
        compiler_params=pltpu.CompilerParams(
            collective_id=0, has_side_effects=True, vmem_limit_bytes=56 << 20),
    )(genotypes, kin_diag, kin_blocks, kin_pairs, pair_count, gene_counts)


def solution(mesh):
    placed = (P("people", "var"), P("people", None, None), P("people", None, None), P(), P(), P())
    return jax.shard_map(
        functools.partial(body, mesh.shape["people"], mesh.shape["var"]),
        mesh=mesh, in_specs=placed, out_specs=P(("var", "people"), None), check_vma=False,
    )
```

time: 320 us -> 99.9 us (0.31); the launches traced: 316 us -> 99.7 us
  waiting for transfers between devices: 195 us -> 0 us
  Pallas kernels: 0 us -> 96.3 us
  local copies, waits for them, and re-layouts: 75.3 us -> 3.35 us
  matrix products: 29.9 us -> 0 us
  between operations: 13.2 us -> 0.01 us
    all_gather x2 -> x0, waiting for transfers between devices: 107 us -> none  [the longest x1 72.1 us: body(): shard_rows = lax.all_gather(genotypes, 'people', axis=0, tiled=True)]
    pallas_call x0 -> x1, Pallas kernels: none -> 96.3 us  [body(): pl.pallas_call(functools.partial(kernel, people, var), out_shape=jax.Shap...]
    reduce_scatter x1 -> x0, waiting for transfers between devices: 87.3 us -> none  [body(): lax.psum_scatter(partial_value, 'people', scatter_dimension=0, tiled=True)]
    gather x2 -> x0, local copies, waits for them, and re-layouts: 48.6 us -> none  [body(): jnp.take(shard_rows, jnp.clip(wanted, 0, row_span - 1).reshape(-1), axis=0)]
    dot_general x5 -> x0, matrix products: 29.9 us -> none  [the longest x1 12.7 us: body(): jnp.einsum('jab,jbv->jav', kin_blocks, fetched, preferred_element_type=jn...]
    dot_general x1 -> x0, local copies, waits for them, and re-layouts: 20.3 us -> none  [body(): jnp.einsum('jab,jbv->jav', kin_blocks, fetched, preferred_element_type=jn...]
  transfers between devices with their start and end apart: 3 -> 0, of which waited for: 3 -> 0; matrix products, arithmetic and copies ran while one was open for 1% -> 0% of each run, Pallas kernels for 0% -> 0%
where the time goes in v1:
time: 99.9 us; the launch traced here: 99.7 us
  Pallas kernels  96.3 us (96%)
  local copies, waits for them, and re-layouts  3.35 us (3%)
    pallas_call x1, Pallas kernels, body(): pl.pallas_call(functools.partial(kernel, people, var), out_shape=jax.Shap...  96.3 us
    unnamed x2, local copies, waits for them, and re-layouts  3.35 us

profile of v1, /device:TPU:26, one launch (start us, length us, event | category | flops | bytes accessed | tf_op | source)
XLA Modules:
  0.0 99.7 jit_solution(17831360585286683739)
XLA Ops:
  0.0 1.5 %copy.7.pairs_hbm = s32[256,2]{1,0:T(8,128)} copy(s32[256,2]{0,1:T(2,128)} %param.9) | data formatting | bytes 4096 | tf_op args[3]
  1.5 96.3 %shard_map.64 = f32[64,2048]{1,0:T(8,128)} custom-call(bf16[512,512]{1,0:T(8,128)(2,1)} %g_ref.1, bf16[2,256,256]{2,1,0:T(8,128)(2,1)} %kd_hbm.1, bf16[32,256,256]{2,1,0:T(8,128)(2,1)} %kb_hbm.1, s32[256,2]{1,0:T(8,128)} %copy.7.pairs_hbm, s32[8]{0:T(128)} %cnt_ref.1, s32[64]{0:T(128)} %gc_ref.1), custom_call_target="tpu_custom_call" | custom-call | tf_op jit(solution)/shard_map/pallas_call | solution.py:219
  97.8 1.9 %copy.9 = f32[64,2048]{1,0:T(8,128)} copy(f32[64,2048]{1,0:T(8,128)} %shard_map.64) | data formatting | bytes 1048576

commit v2 on v1

v2 whole, which is shorter than its diff:
```python
import functools
import math

import jax
import jax.numpy as jnp
from jax import lax
from jax.experimental import pallas as pl
from jax.experimental.pallas import tpu as pltpu
from jax.sharding import PartitionSpec as P

BLOCK = 256
SUB = 2
CORES = 2
MESH = pl.DeviceIdType.MESH


def ring_place(index, nz, nx):
    z, x = index // nx, index % nx
    back = nz - 1 - z
    along = jnp.where(back % 2 == 0, x - 1, nx - 1 - x)
    return jnp.where(x == 0, z, nz + back * (nx - 1) + along)


def ring_index(place, nz, nx):
    rest = jnp.where(place < nz, 0, place - nz)
    back, along = rest // (nx - 1), rest % (nx - 1)
    x = jnp.where(back % 2 == 0, 1 + along, nx - 1 - along)
    return jnp.where(place < nz, place * nx, (nz - 1 - back) * nx + x)


def kernel(people, var, g_ref, kd_hbm, kb_hbm, pairs_ref, cnt_ref, gc_ref, out_ref,
           gall_a, gall_b, gvar, krv_a, krv_b, kd, kb, acc, g_t, kr_t, pbuf, rbuf, rid, cid,
           ring_send, ring_recv, var_send, var_recv, sum_send, sum_recv, load_sem):
    rows, cols = g_ref.shape
    wide = cols // 2
    nx = math.isqrt(people // 2)
    nz = people // nx
    ny = var // CORES
    slots = kb.shape[0]
    galls, krvs = (gall_a, gall_b), (krv_a, krv_b)
    me, q = lax.axis_index("people"), lax.axis_index("var")
    y, core = q // CORES, q % CORES
    other = y * CORES + (CORES - 1 - core)

    loads = [
        pltpu.make_async_copy(kd_hbm, kd, load_sem.at[0]),
        pltpu.make_async_copy(kb_hbm, kb, load_sem.at[1]),
    ]
    for load in loads:
        load.start()

    barrier = pltpu.get_barrier_semaphore()
    for step in range(1, people):
        pl.semaphore_signal(barrier, inc=1, device_id=(lax.rem(me + step, people), q), device_id_type=MESH)
    for step in range(1, var):
        pl.semaphore_signal(barrier, inc=1, device_id=(me, lax.rem(q + step, var)), device_id_type=MESH)

    for h in range(2):
        for half in range(2):
            galls[h][2 * me + half] = g_ref[pl.ds(half * BLOCK, BLOCK), h * wide:(h + 1) * wide]
    gvar[q] = g_ref[...]
    pl.semaphore_wait(barrier, people + var - 2)

    place = ring_place(me, nz, nx)
    right = ring_index(lax.rem(place + 1, people), nz, nx)
    left = ring_index(lax.rem(place + people - 1, people), nz, nx)
    part = BLOCK // SUB

    def ring_copy(h, step, way, sub):
        shift = people - step if way == 0 else step
        source = ring_index(lax.rem(place + shift, people), nz, nx)
        view = galls[h].at[2 * source + way, pl.ds(sub * part, part)]
        return pltpu.make_async_remote_copy(
            src_ref=view, dst_ref=view,
            send_sem=ring_send.at[h, step, way, sub], recv_sem=ring_recv.at[h, step, way, sub],
            device_id=(right if way == 0 else left, q), device_id_type=MESH)

    def ring_start(h):
        for sub in range(SUB):
            for way in range(2):
                ring_copy(h, 0, way, sub).start()

    def ring_step(h, step):
        for sub in range(SUB):
            for way in range(2):
                ring_copy(h, step - 1, way, sub).wait_recv()
                ring_copy(h, step, way, sub).start()

    def ring_last(h):
        for sub in range(SUB):
            for way in range(2):
                ring_copy(h, people - 2, way, sub).wait_recv()

    def var_copy(buf, use, slot, target, sem):
        return pltpu.make_async_remote_copy(
            src_ref=buf.at[slot], dst_ref=buf.at[slot],
            send_sem=var_send.at[use, sem], recv_sem=var_recv.at[use, sem],
            device_id=(me, target), device_id_type=MESH)

    def var_first(buf, use):
        for dy in range(1, ny):
            var_copy(buf, use, q, lax.rem(y + dy, ny) * CORES + core, dy - 1).start()
        var_copy(buf, use, q, other, ny - 1).start()

    def var_forward(buf, use):
        for dy in range(1, ny):
            slot = lax.rem(y + ny - dy, ny) * CORES + core
            var_copy(buf, use, slot, other, dy - 1).wait_recv()
            var_copy(buf, use, slot, other, ny - 1 + dy).start()

    def var_finish(buf, use):
        for sem in range(ny - 1, 2 * ny - 1):
            var_copy(buf, use, q, other, sem).wait_recv()
        for sem in range(2 * ny - 1):
            var_copy(buf, use, q, other, sem).wait_send()

    def gene_step(gene, end):
        end = end + gc_ref[gene]
        row_ids = q * cols + lax.broadcasted_iota(jnp.int32, rid.shape, 0)
        col_ids = lax.broadcasted_iota(jnp.int32, cid.shape, 1)
        rid[...] += (row_ids >= end).astype(jnp.int32)
        cid[...] += (col_ids >= end).astype(jnp.int32)
        return end

    def diag_terms(h):
        for half in range(2):
            acc[half] = jnp.dot(
                kd[half], g_ref[pl.ds(half * BLOCK, BLOCK), h * wide:(h + 1) * wide],
                preferred_element_type=jnp.float32)

    def pair_terms(h, first, last):
        def pair_step(slot, carry):
            row = pairs_ref[0, me * slots + slot] - me * 2
            col = pairs_ref[1, me * slots + slot]
            live = slot < cnt_ref[me]
            term = jnp.dot(kb[slot], galls[h][col], preferred_element_type=jnp.float32)
            for half in range(2):
                weight = jnp.where(live & (row == half), 1.0, 0.0).astype(jnp.float32)
                acc[half] += term * weight
            return carry

        lax.fori_loop(first, last, pair_step, 0)

    def kin_out(h):
        for half in range(2):
            krvs[h][q, pl.ds(half * BLOCK, BLOCK), :] = acc[half].astype(jnp.bfloat16)
        var_first(krvs[h], 1 + h)
        kr_t[h * wide:(h + 1) * wide, :] = krvs[h][q].T

    ring_start(0)
    var_first(gvar, 0)
    rid[...] = jnp.zeros_like(rid)
    cid[...] = jnp.zeros_like(cid)
    genes = gc_ref.shape[0]
    share = pl.cdiv(genes, people - 2)

    def first_half(step, end):
        ring_step(0, step)
        begin = (step - 1) * share
        return lax.fori_loop(jnp.minimum(begin, genes), jnp.minimum(begin + share, genes), gene_step, end)

    lax.fori_loop(1, people - 1, first_half, jnp.int32(0))
    ring_start(1)
    g_t[...] = g_ref[...].T
    for load in loads:
        load.wait()
    diag_terms(0)
    ring_last(0)

    busy = 4
    some = slots // busy

    def second_half(step, carry):
        ring_step(1, step)
        pair_terms(0, (step - 1) * some, step * some)
        return carry

    lax.fori_loop(1, busy + 1, second_half, 0)
    kin_out(0)

    def second_rest(step, carry):
        ring_step(1, step)
        return carry

    lax.fori_loop(busy + 1, people - 1, second_rest, 0)
    var_forward(gvar, 0)
    diag_terms(1)
    ring_last(1)
    var_forward(krvs[0], 1)
    pair_terms(1, 0, slots)
    kin_out(1)

    def ring_drain(step, carry):
        for h in range(2):
            for sub in range(SUB):
                for way in range(2):
                    ring_copy(h, step, way, sub).wait_send()
        return carry

    lax.fori_loop(0, people - 1, ring_drain, 0)
    var_finish(gvar, 0)
    var_finish(krvs[0], 1)
    var_forward(krvs[1], 2)
    var_finish(krvs[1], 2)

    width = pbuf.shape[2]
    chunk = rows // people
    tile = BLOCK
    per_tile = tile // chunk

    def sum_copy(target):
        return pltpu.make_async_remote_copy(
            src_ref=pbuf.at[target], dst_ref=rbuf.at[me],
            send_sem=sum_send.at[target], recv_sem=sum_recv.at[me],
            device_id=(target, q), device_id_type=MESH)

    for t in range(cols // tile):
        span = pl.ds(t * tile, tile)
        row_gene = rid[span, 0:1]
        for j in range(var // 2):
            for h in range(2):
                total = jnp.zeros((tile, wide), jnp.float32)
                for k in (j, j + var // 2):
                    value = jnp.dot(g_t[span, :], krvs[h][k], preferred_element_type=jnp.float32)
                    value += jnp.dot(
                        kr_t[span, :], gvar[k, :, h * wide:(h + 1) * wide], preferred_element_type=jnp.float32)
                    same = row_gene == cid[0:1, k * cols + h * wide:k * cols + (h + 1) * wide]
                    total = jnp.where(same, value, total)
                at = j * cols + h * wide
                pbuf[t * per_tile:(t + 1) * per_tile, :, at:at + wide] = (
                    total.astype(jnp.bfloat16).reshape(per_tile, chunk, wide))
        for k in range(per_tile):
            target = t * per_tile + k

            @pl.when(target != me)
            def _():
                sum_copy(target).start()

    own = rid[pl.ds(me * chunk, chunk), 0:1]
    final = pbuf[me].astype(jnp.float32)
    for step in range(1, people):
        source = lax.rem(me + step, people)
        pltpu.make_async_remote_copy(
            src_ref=pbuf.at[source], dst_ref=rbuf.at[source],
            send_sem=sum_send.at[source], recv_sem=sum_recv.at[source],
            device_id=(source, q), device_id_type=MESH).wait_recv()
        final += rbuf[source].astype(jnp.float32)
    final = final * (0.5 / math.sqrt(rows * people))
    for k in range(2):
        same = own == cid[0:1, k * width:(k + 1) * width]
        out_ref[:, k * width:(k + 1) * width] = jnp.where(same, final, 0.0)
    for step in range(1, people):
        sum_copy(lax.rem(me + step, people)).wait_send()


def body(people, var, genotypes, kin_diag, kin_blocks, kin_pairs, pair_count, gene_counts):
    rows, cols = genotypes.shape
    total = cols * var
    chunk = rows // people
    ny = var // CORES
    bf16, f32 = jnp.bfloat16, jnp.float32
    anywhere = pl.BlockSpec(memory_space=pl.ANY)
    vmem = pl.BlockSpec(memory_space=pltpu.VMEM)
    smem = pl.BlockSpec(memory_space=pltpu.SMEM)
    dma = pltpu.SemaphoreType.DMA
    return pl.pallas_call(
        functools.partial(kernel, people, var),
        out_shape=jax.ShapeDtypeStruct((chunk, total), f32),
        in_specs=[vmem, anywhere, anywhere, smem, smem, smem],
        out_specs=vmem,
        scratch_shapes=[
            pltpu.VMEM((2 * people, BLOCK, cols // 2), bf16),
            pltpu.VMEM((2 * people, BLOCK, cols // 2), bf16),
            pltpu.VMEM((var, rows, cols), bf16),
            pltpu.VMEM((var, rows, cols // 2), bf16),
            pltpu.VMEM((var, rows, cols // 2), bf16),
            pltpu.VMEM(kin_diag.shape, bf16),
            pltpu.VMEM(kin_blocks.shape, bf16),
            pltpu.VMEM((2, BLOCK, cols // 2), f32),
            pltpu.VMEM((cols, rows), bf16),
            pltpu.VMEM((cols, rows), bf16),
            pltpu.VMEM((people, chunk, total // 2), bf16),
            pltpu.VMEM((people, chunk, total // 2), bf16),
            pltpu.VMEM((cols, 128), jnp.int32),
            pltpu.VMEM((8, total), jnp.int32),
            dma((2, people - 1, 2, SUB)),
            dma((2, people - 1, 2, SUB)),
            dma((3, 2 * ny - 1)),
            dma((3, 2 * ny - 1)),
            dma((people,)),
            dma((people,)),
            dma((2,)),
        ],
        compiler_params=pltpu.CompilerParams(
            collective_id=0, has_side_effects=True, vmem_limit_bytes=56 << 20),
    )(genotypes, kin_diag, kin_blocks, kin_pairs.T, pair_count, gene_counts)


def solution(mesh):
    placed = (P("people", "var"), P("people", None, None), P("people", None, None), P(), P(), P())
    return jax.shard_map(
        functools.partial(body, mesh.shape["people"], mesh.shape["var"]),
        mesh=mesh, in_specs=placed, out_specs=P(("var", "people"), None), check_vma=False,
    )
```

time: 99.9 us -> 101 us (1.011)
  Pallas kernels: 96.3 us -> 98.5 us
  local copies, waits for them, and re-layouts: 3.35 us -> 1.87 us
    pallas_call x1, Pallas kernels: 96.3 us -> 98.5 us  [body(): pl.pallas_call(functools.partial(kernel, people, var), out_shape=jax.Shap...]
    unnamed x2 -> x1, local copies, waits for them, and re-layouts: 3.35 us -> 1.87 us
where the time goes in v2:
time: 101 us; the launch traced here: 100 us
  Pallas kernels  98.5 us (98%)
  local copies, waits for them, and re-layouts  1.87 us (2%)
    pallas_call x1, Pallas kernels, body(): pl.pallas_call(functools.partial(kernel, people, var), out_shape=jax.Shap...  98.5 us

profile of v2, /device:TPU:26, one launch (start us, length us, event | category | flops | bytes accessed | tf_op | source)
XLA Modules:
  0.0 100.3 jit_solution(11885200782344959773)
XLA Ops:
  0.0 98.5 %shard_map.64 = f32[64,2048]{1,0:T(8,128)} custom-call(bf16[512,512]{1,0:T(8,128)(2,1)} %g_ref.1, bf16[2,256,256]{2,1,0:T(8,128)(2,1)} %kd_hbm.1, bf16[32,256,256]{2,1,0:T(8,128)(2,1)} %kb_hbm.1, s32[2,256]{1,0:T(2,128)} %bitcast.1, s32[8]{0:T(128)} %cnt_ref.1, s32[64]{0:T(128)} %gc_ref.1), custom_call_target="tpu_custom_call" | custom-call | tf_op jit(solution)/shard_map/pallas_call | solution.py:266
  98.5 1.9 %copy.8 = f32[64,2048]{1,0:T(8,128)} copy(f32[64,2048]{1,0:T(8,128)} %shard_map.64) | data formatting | bytes 1048576

commit v3 on v2

--- a/solution.py
+++ b/solution.py
@@ -9,7 +9,7 @@
 from jax.sharding import PartitionSpec as P
 
 BLOCK = 256
-SUB = 2
+SUB = 4
 CORES = 2
 MESH = pl.DeviceIdType.MESH
 
@@ -80,11 +80,13 @@
             for way in range(2):
                 ring_copy(h, 0, way, sub).start()
 
-    def ring_step(h, step):
+    def ring_step(h, step, work, carry):
         for sub in range(SUB):
             for way in range(2):
                 ring_copy(h, step - 1, way, sub).wait_recv()
                 ring_copy(h, step, way, sub).start()
+                carry = work(((step - 1) * SUB + sub) * 2 + way, carry)
+        return carry
 
     def ring_last(h):
         for sub in range(SUB):
@@ -128,18 +130,19 @@
                 kd[half], g_ref[pl.ds(half * BLOCK, BLOCK), h * wide:(h + 1) * wide],
                 preferred_element_type=jnp.float32)
 
-    def pair_terms(h, first, last):
-        def pair_step(slot, carry):
+    def pair_terms(h, first, count):
+        picks, lefts = [], ([], [])
+        for slot in (first + k for k in range(count)):
             row = pairs_ref[0, me * slots + slot] - me * 2
-            col = pairs_ref[1, me * slots + slot]
             live = slot < cnt_ref[me]
-            term = jnp.dot(kb[slot], galls[h][col], preferred_element_type=jnp.float32)
+            picks.append(galls[h][pairs_ref[1, me * slots + slot]])
             for half in range(2):
-                weight = jnp.where(live & (row == half), 1.0, 0.0).astype(jnp.float32)
-                acc[half] += term * weight
-            return carry
-
-        lax.fori_loop(first, last, pair_step, 0)
+                weight = jnp.where(live & (row == half), 1.0, 0.0).astype(jnp.bfloat16)
+                lefts[half].append(kb[slot] * weight)
+        picks = jnp.concatenate(picks, axis=0)
+        for half in range(2):
+            acc[half] += jnp.dot(
+                jnp.concatenate(lefts[half], axis=1), picks, preferred_element_type=jnp.float32)
 
     def kin_out(h):
         for half in range(2):
@@ -152,14 +155,13 @@
     rid[...] = jnp.zeros_like(rid)
     cid[...] = jnp.zeros_like(cid)
     genes = gc_ref.shape[0]
-    share = pl.cdiv(genes, people - 2)
-
-    def first_half(step, end):
-        ring_step(0, step)
-        begin = (step - 1) * share
+    share = pl.cdiv(genes, (people - 2) * 2 * SUB)
+
+    def some_genes(turn, end):
+        begin = turn * share
         return lax.fori_loop(jnp.minimum(begin, genes), jnp.minimum(begin + share, genes), gene_step, end)
 
-    lax.fori_loop(1, people - 1, first_half, jnp.int32(0))
+    lax.fori_loop(1, people - 1, lambda step, end: ring_step(0, step, some_genes, end), jnp.int32(0))
     ring_start(1)
     g_t[...] = g_ref[...].T
     for load in loads:
@@ -168,57 +170,48 @@
     ring_last(0)
 
     busy = 4
-    some = slots // busy
-
-    def second_half(step, carry):
-        ring_step(1, step)
-        pair_terms(0, (step - 1) * some, step * some)
-        return carry
-
-    lax.fori_loop(1, busy + 1, second_half, 0)
+    some = slots // (busy * 2 * SUB)
+
+    def some_pairs(turn, carry):
+        pair_terms(0, turn * some, some)
+        return carry
+
+    def no_work(turn, carry):
+        return carry
+
+    lax.fori_loop(1, busy + 1, lambda step, carry: ring_step(1, step, some_pairs, carry), 0)
     kin_out(0)
 
-    def second_rest(step, carry):
-        ring_step(1, step)
-        return carry
-
-    lax.fori_loop(busy + 1, people - 1, second_rest, 0)
+    lax.fori_loop(busy + 1, people - 1, lambda step, carry: ring_step(1, step, no_work, carry), 0)
     var_forward(gvar, 0)
     diag_terms(1)
     ring_last(1)
     var_forward(krvs[0], 1)
-    pair_terms(1, 0, slots)
+
+    def group_step(group, carry):
+        pair_terms(1, group * 4, 4)
+        return carry
+
+    lax.fori_loop(0, slots // 4, group_step, 0)
     kin_out(1)
-
-    def ring_drain(step, carry):
-        for h in range(2):
-            for sub in range(SUB):
-                for way in range(2):
-                    ring_copy(h, step, way, sub).wait_send()
-        return carry
-
-    lax.fori_loop(0, people - 1, ring_drain, 0)
     var_finish(gvar, 0)
     var_finish(krvs[0], 1)
-    var_forward(krvs[1], 2)
-    var_finish(krvs[1], 2)
-
-    width = pbuf.shape[2]
+
     chunk = rows // people
     tile = BLOCK
     per_tile = tile // chunk
 
-    def sum_copy(target):
+    def sum_copy(h, target):
         return pltpu.make_async_remote_copy(
-            src_ref=pbuf.at[target], dst_ref=rbuf.at[me],
-            send_sem=sum_send.at[target], recv_sem=sum_recv.at[me],
+            src_ref=pbuf.at[h, target], dst_ref=rbuf.at[h, me],
+            send_sem=sum_send.at[h, target], recv_sem=sum_recv.at[h, me],
             device_id=(target, q), device_id_type=MESH)
 
-    for t in range(cols // tile):
-        span = pl.ds(t * tile, tile)
-        row_gene = rid[span, 0:1]
-        for j in range(var // 2):
-            for h in range(2):
+    def sums(h):
+        for t in range(cols // tile):
+            span = pl.ds(t * tile, tile)
+            row_gene = rid[span, 0:1]
+            for j in range(var // 2):
                 total = jnp.zeros((tile, wide), jnp.float32)
                 for k in (j, j + var // 2):
                     value = jnp.dot(g_t[span, :], krvs[h][k], preferred_element_type=jnp.float32)
@@ -226,31 +219,47 @@
                         kr_t[span, :], gvar[k, :, h * wide:(h + 1) * wide], preferred_element_type=jnp.float32)
                     same = row_gene == cid[0:1, k * cols + h * wide:k * cols + (h + 1) * wide]
                     total = jnp.where(same, value, total)
-                at = j * cols + h * wide
-                pbuf[t * per_tile:(t + 1) * per_tile, :, at:at + wide] = (
+                pbuf[h, t * per_tile:(t + 1) * per_tile, :, j * wide:(j + 1) * wide] = (
                     total.astype(jnp.bfloat16).reshape(per_tile, chunk, wide))
-        for k in range(per_tile):
-            target = t * per_tile + k
-
-            @pl.when(target != me)
-            def _():
-                sum_copy(target).start()
+            for k in range(per_tile):
+                target = t * per_tile + k
+
+                @pl.when(target != me)
+                def _():
+                    sum_copy(h, target).start()
+
+    sums(0)
+    var_forward(krvs[1], 2)
+
+    def ring_drain(step, carry):
+        for h in range(2):
+            for sub in range(SUB):
+                for way in range(2):
+                    ring_copy(h, step, way, sub).wait_send()
+        return carry
+
+    lax.fori_loop(0, people - 1, ring_drain, 0)
+    var_finish(krvs[1], 2)
+    sums(1)
 
     own = rid[pl.ds(me * chunk, chunk), 0:1]
-    final = pbuf[me].astype(jnp.float32)
-    for step in range(1, people):
-        source = lax.rem(me + step, people)
-        pltpu.make_async_remote_copy(
-            src_ref=pbuf.at[source], dst_ref=rbuf.at[source],
-            send_sem=sum_send.at[source], recv_sem=sum_recv.at[source],
-            device_id=(source, q), device_id_type=MESH).wait_recv()
-        final += rbuf[source].astype(jnp.float32)
-    final = final * (0.5 / math.sqrt(rows * people))
-    for k in range(2):
-        same = own == cid[0:1, k * width:(k + 1) * width]
-        out_ref[:, k * width:(k + 1) * width] = jnp.where(same, final, 0.0)
-    for step in range(1, people):
-        sum_copy(lax.rem(me + step, people)).wait_send()
+    for h in range(2):
+        final = pbuf[h, me].astype(jnp.float32)
+        for step in range(1, people):
+            source = lax.rem(me + step, people)
+            pltpu.make_async_remote_copy(
+                src_ref=pbuf.at[h, source], dst_ref=rbuf.at[h, source],
+                send_sem=sum_send.at[h, source], recv_sem=sum_recv.at[h, source],
+                device_id=(source, q), device_id_type=MESH).wait_recv()
+            final += rbuf[h, source].astype(jnp.float32)
+        final = final * (0.5 / math.sqrt(rows * people))
+        for k in range(var):
+            at, j = k * cols + h * wide, k % (var // 2)
+            same = own == cid[0:1, at:at + wide]
+            out_ref[:, at:at + wide] = jnp.where(same, final[:, j * wide:(j + 1) * wide], 0.0)
+    for h in range(2):
+        for step in range(1, people):
+            sum_copy(h, lax.rem(me + step, people)).wait_send()
 
 
 def body(people, var, genotypes, kin_diag, kin_blocks, kin_pairs, pair_count, gene_counts):
@@ -279,16 +288,16 @@
             pltpu.VMEM((2, BLOCK, cols // 2), f32),
             pltpu.VMEM((cols, rows), bf16),
             pltpu.VMEM((cols, rows), bf16),
-            pltpu.VMEM((people, chunk, total // 2), bf16),
-            pltpu.VMEM((people, chunk, total // 2), bf16),
+            pltpu.VMEM((2, people, chunk, total // 4), bf16),
+            pltpu.VMEM((2, people, chunk, total // 4), bf16),
             pltpu.VMEM((cols, 128), jnp.int32),
             pltpu.VMEM((8, total), jnp.int32),
             dma((2, people - 1, 2, SUB)),
             dma((2, people - 1, 2, SUB)),
             dma((3, 2 * ny - 1)),
             dma((3, 2 * ny - 1)),
-            dma((people,)),
-            dma((people,)),
+            dma((2, people)),
+            dma((2, people)),
             dma((2,)),
         ],
         compiler_params=pltpu.CompilerParams(

time: 101 us -> 83 us (0.82)
  Pallas kernels: 98.5 us -> 80.9 us
    pallas_call x1, Pallas kernels: 98.5 us -> 80.9 us  [body(): pl.pallas_call(functools.partial(kernel, people, var), out_shape=jax.Shap...]
where the time goes in v3:
time: 83 us; the launch traced here: 82.8 us
  Pallas kernels  80.9 us (97%)
  local copies, waits for them, and re-layouts  1.87 us (2%)
    pallas_call x1, Pallas kernels, body(): pl.pallas_call(functools.partial(kernel, people, var), out_shape=jax.Shap...  80.9 us
    unnamed x1, local copies, waits for them, and re-layouts  1.87 us

profile of v3, /device:TPU:26, one launch (start us, length us, event | category | flops | bytes accessed | tf_op | source)
XLA Modules:
  0.0 82.8 jit_solution(7586161009721581450)
XLA Ops:
  0.0 80.9 %shard_map.64 = f32[64,2048]{1,0:T(8,128)} custom-call(bf16[512,512]{1,0:T(8,128)(2,1)} %g_ref.1, bf16[2,256,256]{2,1,0:T(8,128)(2,1)} %kd_hbm.1, bf16[32,256,256]{2,1,0:T(8,128)(2,1)} %kb_hbm.1, s32[2,256]{1,0:T(2,128)} %bitcast.1, s32[8]{0:T(128)} %cnt_ref.1, s32[64]{0:T(128)} %gc_ref.1), custom_call_target="tpu_custom_call" | custom-call | tf_op jit(solution)/shard_map/pallas_call | solution.py:275
  80.9 1.9 %copy.8 = f32[64,2048]{1,0:T(8,128)} copy(f32[64,2048]{1,0:T(8,128)} %shard_map.64) | data formatting | bytes 1048576

commit v4 on v3

--- a/solution.py
+++ b/solution.py
@@ -9,7 +9,7 @@
 from jax.sharding import PartitionSpec as P
 
 BLOCK = 256
-SUB = 4
+SUB = 8
 CORES = 2
 MESH = pl.DeviceIdType.MESH
 
@@ -169,7 +169,7 @@
     diag_terms(0)
     ring_last(0)
 
-    busy = 4
+    busy = 2
     some = slots // (busy * 2 * SUB)
 
     def some_pairs(turn, carry):

time: 83 us -> 82.1 us (0.989)
  Pallas kernels: 80.9 us -> 80 us
    pallas_call x1, Pallas kernels: 80.9 us -> 80 us  [body(): pl.pallas_call(functools.partial(kernel, people, var), out_shape=jax.Shap...]
where the time goes in v4:
time: 82.1 us; the launch traced here: 81.9 us
  Pallas kernels  80 us (97%)
  local copies, waits for them, and re-layouts  1.87 us (2%)
    pallas_call x1, Pallas kernels, body(): pl.pallas_call(functools.partial(kernel, people, var), out_shape=jax.Shap...  80 us
    unnamed x1, local copies, waits for them, and re-layouts  1.87 us

profile of v4, /device:TPU:26, one launch (start us, length us, event | category | flops | bytes accessed | tf_op | source)
XLA Modules:
  0.0 81.9 jit_solution(16891876170827779838)
XLA Ops:
  0.0 80.0 %shard_map.64 = f32[64,2048]{1,0:T(8,128)} custom-call(bf16[512,512]{1,0:T(8,128)(2,1)} %g_ref.1, bf16[2,256,256]{2,1,0:T(8,128)(2,1)} %kd_hbm.1, bf16[32,256,256]{2,1,0:T(8,128)(2,1)} %kb_hbm.1, s32[2,256]{1,0:T(2,128)} %bitcast.1, s32[8]{0:T(128)} %cnt_ref.1, s32[64]{0:T(128)} %gc_ref.1), custom_call_target="tpu_custom_call" | custom-call | tf_op jit(solution)/shard_map/pallas_call | solution.py:275
  80.0 1.9 %copy.8 = f32[64,2048]{1,0:T(8,128)} copy(f32[64,2048]{1,0:T(8,128)} %shard_map.64) | data formatting | bytes 1048576
